TPU v7x, 32 devices: a whole 2x2x4 slice. The times are simulated.
32 devices in a mesh: dp: 16 (over z, y, core), seq: 2 (over x).
Axes of the slice: x: 2, y: 2, z: 4, core: 2. Of those that a mesh axis runs over, the one named last changes fastest.
Arguments:
- latents: bfloat16 [2, 16, 1024, 1152], P(None, 'dp', 'seq'), may hold values from -6 to 6
- cond: float32 [24, 1152], replicated, may hold values from -6 to 6
- slot_mask: int32 [2, 16], replicated, may hold values from 0 to 1, as said below
- slot_image: int32 [2, 16], replicated, may hold values from 0 to 23, as said below
- teacher: bfloat16 [2, 16, 1024, 1152], P(None, 'dp', 'seq'), may hold values from -6 to 6
- cotangent: bfloat16 [2, 16, 1024, 1152], P(None, 'dp', 'seq'), may hold values from -6 to 6
- ada_w: bfloat16 [1152, 6912], P('dp', 'seq'), may hold values from -0.1875 to 0.1875
- ada_b: float32 [6912], replicated, may hold values from -3 to 3
- qkv_w: bfloat16 [1152, 3456], P('dp', 'seq'), may hold values from -0.1875 to 0.1875
- qv_b: float32 [2304], replicated, may hold values from -2 to 2
- proj_w: bfloat16 [1152, 1152], P('dp', 'seq'), may hold values from -1.5 to 1.5
- proj_b: float32 [1152], replicated, may hold values from -2 to 2
- fc1_w: bfloat16 [1152, 4608], P('dp', 'seq'), may hold values from -0.1875 to 0.1875
- fc1_b: float32 [4608], replicated, may hold values from -2 to 2
- fc2_w: bfloat16 [4608, 1152], P('dp', 'seq'), may hold values from -0.09375 to 0.09375
- fc2_b: float32 [1152], replicated, may hold values from -2 to 2
Outputs:
- block_out: bfloat16 [2, 16, 1024, 1152], P(None, 'dp', 'seq')
- latents_grad: float32 [2, 16, 1024, 1152], P(None, 'dp', 'seq')
- loss: float32 [], replicated
- cond_grad: float32 [24, 1152], replicated
- ada_w_grad: float32 [1152, 6912], P('dp', 'seq')
- ada_b_grad: float32 [6912], replicated
- qkv_w_grad: float32 [1152, 3456], P('dp', 'seq')
- qv_b_grad: float32 [2304], replicated
- proj_w_grad: float32 [1152, 1152], P('dp', 'seq')
- proj_b_grad: float32 [1152], replicated
- fc1_w_grad: float32 [1152, 4608], P('dp', 'seq')
- fc1_b_grad: float32 [4608], replicated
- fc2_w_grad: float32 [4608, 1152], P('dp', 'seq')
- fc2_b_grad: float32 [1152], replicated
Inputs may be any that keep to these rules, and one draw needn't show every extreme that they name: Micro-batch i holds the images n with n mod 2 = i, each in exactly one slot with slot_mask 1; all other slots have slot_mask 0. `slot_image`: in a slot with slot_mask 1, the image it holds; in a pad slot any image number.
All inputs are finite; a program needn't handle non-finite values.
Results may differ from a plain program's by a relative error of at most 0.018.
The roundings to bfloat16 on the way count: a program that leaves them out, or rounds other values in their place, can miss the bound.
Values may be sent and summed in bfloat16 or wider, within the bound.
A program may use at most 448 MiB of HBM per device.

v0:
```python
import jax
import jax.numpy as jnp
from jax import lax
from jax.sharding import PartitionSpec as P

HEADS = 16
HIGH = lax.Precision.HIGHEST


def layer_norm(value):
    center = value - jnp.mean(value, axis=-1, keepdims=True)
    spread = jnp.mean(center * center, axis=-1, keepdims=True)
    return center * lax.rsqrt(spread + 1e-06)


def gelu_tanh(value):
    return jax.nn.gelu(value, approximate=True)


def local(
    latents,
    cond,
    slot_mask,
    slot_image,
    teacher,
    cotangent,
    ada_w,
    ada_b,
    qkv_w,
    qv_b,
    proj_w,
    proj_b,
    fc1_w,
    fc1_b,
    fc2_w,
    fc2_b,
):
    f32 = jnp.float32
    bf16 = jnp.bfloat16
    micro = latents.shape[0]
    slots_dev = latents.shape[1]
    local_len = latents.shape[2]
    width = latents.shape[3]
    images = cond.shape[0]
    heads = HEADS
    head_size = width // heads
    full_len = local_len * lax.axis_size("seq")
    hidden_units = fc1_b.shape[0]
    scale = head_size ** (-0.5)
    dp_index = lax.axis_index("dp")
    seq_index = lax.axis_index("seq")
    mod_cols = ada_w.shape[1]
    col_start = seq_index * mod_cols
    count = jnp.sum(slot_mask).astype(f32) * full_len
    divisor = count * width
    image_table = jnp.arange(images, dtype=jnp.int32)
    grad_qkv = jnp.zeros((width, 3 * width), f32)
    grad_proj = jnp.zeros((width, width), f32)
    grad_fc1 = jnp.zeros((width, hidden_units), f32)
    grad_fc2 = jnp.zeros((hidden_units, width), f32)
    grad_ada = jnp.zeros((width, mod_cols), f32)
    grad_cond = jnp.zeros((images, width), f32)
    bias_ada = jnp.zeros((6 * width,), f32)
    bias_qv = jnp.zeros((2 * width,), f32)
    bias_proj = jnp.zeros((width,), f32)
    bias_fc1 = jnp.zeros((hidden_units,), f32)
    bias_fc2 = jnp.zeros((width,), f32)
    loss_sum = jnp.zeros((), f32)
    column_ids = jnp.arange(6 * width, dtype=jnp.int32)
    in_mine = (column_ids >= col_start) & (column_ids < col_start + mod_cols)
    results = []
    input_grads = []
    for micro_index in range(micro):
        qkv_cols = lax.all_gather(qkv_w, "seq", axis=1, tiled=True)
        proj_cols = lax.all_gather(proj_w, "seq", axis=1, tiled=True)
        fc1_cols = lax.all_gather(fc1_w, "seq", axis=1, tiled=True)
        fc2_cols = lax.all_gather(fc2_w, "seq", axis=1, tiled=True)
        qkv_full = lax.all_gather(qkv_cols, "dp", axis=0, tiled=True)
        proj_full = lax.all_gather(proj_cols, "dp", axis=0, tiled=True)
        fc1_full = lax.all_gather(fc1_cols, "dp", axis=0, tiled=True)
        fc2_full = lax.all_gather(fc2_cols, "dp", axis=0, tiled=True)
        ada_cols = lax.all_gather(ada_w, "seq", axis=1, tiled=True)
        ada_full = lax.all_gather(ada_cols, "dp", axis=0, tiled=True)
        qkv_full, proj_full, fc1_full, fc2_full, ada_full = (
            qkv_full,
            proj_full,
            fc1_full,
            fc2_full,
            ada_full,
        )
        image_mine = lax.dynamic_slice_in_dim(
            slot_image[micro_index], dp_index * slots_dev, slots_dev
        )
        mask_mine = lax.dynamic_slice_in_dim(
            slot_mask[micro_index], dp_index * slots_dev, slots_dev
        ).astype(f32)
        pick_mine = (image_mine[:, None] == image_table[None, :]).astype(f32)
        cond_mine = jnp.dot(pick_mine, cond, precision=HIGH)
        silu_mine = jax.nn.silu(cond_mine).astype(bf16)
        modulation = jnp.dot(silu_mine, ada_full, preferred_element_type=f32) + ada_b
        pieces = [
            modulation[:, index * width : (index + 1) * width][:, None, :] for index in range(6)
        ]
        shift1, scale1, gate1, shift2, scale2, gate2 = pieces
        inputs = latents[micro_index].astype(f32)
        normed1 = layer_norm(inputs)
        hidden = (normed1 * (1.0 + scale1) + shift1).astype(bf16)
        joint = jnp.einsum("btd,de->bte", hidden, qkv_full, preferred_element_type=f32)
        query = (joint[..., :width] + qv_b[:width]).astype(bf16)
        keys_local = joint[..., width : 2 * width].astype(bf16)
        values_local = (joint[..., 2 * width :] + qv_b[width:]).astype(bf16)
        keys_all, values_all = (
            lax.all_gather(keys_local, "seq", axis=1, tiled=True),
            lax.all_gather(values_local, "seq", axis=1, tiled=True),
        )
        query_heads = query.reshape(slots_dev, local_len, heads, head_size)
        key_heads = keys_all.reshape(slots_dev, full_len, heads, head_size)
        value_heads = values_all.reshape(slots_dev, full_len, heads, head_size)
        scores = (
            jnp.einsum("bqhe,bkhe->bhqk", query_heads, key_heads, preferred_element_type=f32)
            * scale
        )
        row_top = jnp.max(scores, axis=-1, keepdims=True)
        row_total = jnp.sum(jnp.exp(scores - row_top), axis=-1, keepdims=True)
        probs_low = (jnp.exp(scores - row_top) / row_total).astype(bf16)
        attended = jnp.einsum("bhqk,bkhe->bqhe", probs_low, value_heads, preferred_element_type=f32)
        attended = attended.reshape(slots_dev, local_len, width).astype(bf16)
        branch = jnp.einsum("btd,de->bte", attended, proj_full, preferred_element_type=f32) + proj_b
        middle = inputs + gate1 * branch
        normed2 = layer_norm(middle)
        hidden2 = (normed2 * (1.0 + scale2) + shift2).astype(bf16)
        before = jnp.einsum("btd,df->btf", hidden2, fc1_full, preferred_element_type=f32) + fc1_b
        active = gelu_tanh(before).astype(bf16)
        mlp_out = jnp.einsum("btf,fd->btd", active, fc2_full, preferred_element_type=f32) + fc2_b
        result = middle + gate2 * mlp_out
        results.append(result.astype(bf16))
        valid = mask_mine[:, None, None]
        diff = result - teacher[micro_index].astype(f32)
        loss_sum = loss_sum + jnp.sum(valid * diff * diff)
        grad_out = valid * (2.0 * diff / divisor + cotangent[micro_index].astype(f32))
        d_gate2 = jnp.sum(grad_out * mlp_out, axis=1)
        d_mlp = (grad_out * gate2).astype(bf16)
        grad_fc2 = grad_fc2 + jnp.einsum("btf,btd->fd", active, d_mlp, preferred_element_type=f32)
        bias_fc2 = bias_fc2 + jnp.sum(d_mlp.astype(f32), axis=(0, 1))
        d_active = jnp.einsum("btd,fd->btf", d_mlp, fc2_full, preferred_element_type=f32)
        d_before = jax.vjp(gelu_tanh, before)[1](d_active)[0].astype(bf16)
        grad_fc1 = grad_fc1 + jnp.einsum(
            "btd,btf->df", hidden2, d_before, preferred_element_type=f32
        )
        bias_fc1 = bias_fc1 + jnp.sum(d_before.astype(f32), axis=(0, 1))
        d_hidden2 = jnp.einsum("btf,df->btd", d_before, fc1_full, preferred_element_type=f32)
        d_scale2 = jnp.sum(d_hidden2 * normed2, axis=1)
        d_shift2 = jnp.sum(d_hidden2, axis=1)
        d_middle = grad_out + jax.vjp(layer_norm, middle)[1](d_hidden2 * (1.0 + scale2))[0]
        d_gate1 = jnp.sum(d_middle * branch, axis=1)
        d_branch = (d_middle * gate1).astype(bf16)
        grad_proj = grad_proj + jnp.einsum(
            "btd,bte->de", attended, d_branch, preferred_element_type=f32
        )
        bias_proj = bias_proj + jnp.sum(d_branch.astype(f32), axis=(0, 1))
        d_attended = jnp.einsum(
            "bte,de->btd", d_branch, proj_full, preferred_element_type=f32
        ).astype(bf16)
        d_attended = d_attended.reshape(slots_dev, local_len, heads, head_size)
        again_scores = (
            jnp.einsum("bqhe,bkhe->bhqk", query_heads, key_heads, preferred_element_type=f32)
            * scale
        )
        probs = jnp.exp(again_scores - row_top) / row_total
        d_probs = jnp.einsum("bqhe,bkhe->bhqk", d_attended, value_heads, preferred_element_type=f32)
        row_inner = jnp.sum(probs * d_probs, axis=-1, keepdims=True)
        d_scores = (probs * (d_probs - row_inner)).astype(bf16)
        d_query = (
            jnp.einsum("bhqk,bkhe->bqhe", d_scores, key_heads, preferred_element_type=f32) * scale
        )
        key_terms = (
            jnp.einsum("bhqk,bqhe->bkhe", d_scores, query_heads, preferred_element_type=f32) * scale
        )
        value_terms = jnp.einsum(
            "bhqk,bqhe->bkhe", probs_low, d_attended, preferred_element_type=f32
        )
        key_terms = key_terms.reshape(slots_dev, full_len, width)
        value_terms = value_terms.reshape(slots_dev, full_len, width)
        d_keys, d_values = (
            lax.psum_scatter(
                key_terms.astype(jnp.bfloat16), "seq", scatter_dimension=1, tiled=True
            ).astype(jnp.float32),
            lax.psum_scatter(
                value_terms.astype(jnp.bfloat16), "seq", scatter_dimension=1, tiled=True
            ).astype(jnp.float32),
        )
        d_query = d_query.reshape(slots_dev, local_len, width).astype(bf16)
        d_joint = jnp.concatenate([d_query, d_keys.astype(bf16), d_values.astype(bf16)], axis=-1)
        grad_qkv = grad_qkv + jnp.einsum("btd,bte->de", hidden, d_joint, preferred_element_type=f32)
        bias_qv = bias_qv + jnp.concatenate(
            [
                jnp.sum(d_joint[..., :width].astype(f32), axis=(0, 1)),
                jnp.sum(d_joint[..., 2 * width :].astype(f32), axis=(0, 1)),
            ]
        )
        d_hidden = jnp.einsum("bte,de->btd", d_joint, qkv_full, preferred_element_type=f32)
        d_scale1 = jnp.sum(d_hidden * normed1, axis=1)
        d_shift1 = jnp.sum(d_hidden, axis=1)
        d_inputs = d_middle + jax.vjp(layer_norm, inputs)[1](d_hidden * (1.0 + scale1))[0]
        input_grads.append(d_inputs)
        mod_partial = jnp.concatenate(
            [d_shift1, d_scale1, d_gate1, d_shift2, d_scale2, d_gate2], axis=-1
        )
        d_mod = lax.psum(mod_partial, "seq").astype(bf16)
        own_cols = lax.dynamic_slice_in_dim(d_mod, col_start, mod_cols, 1)
        bias_ada = bias_ada + jnp.where(in_mine, jnp.sum(d_mod.astype(f32), axis=0), 0.0)
        grad_ada = grad_ada + jnp.dot(silu_mine.T, own_cols, preferred_element_type=f32)
        ada_own = lax.dynamic_slice_in_dim(ada_full, col_start, mod_cols, 1)
        d_cond = jnp.einsum("bm,dm->bd", own_cols, ada_own, preferred_element_type=f32)
        d_cond = jax.vjp(jax.nn.silu, cond_mine)[1](d_cond)[0]
        grad_cond = grad_cond + jnp.dot(pick_mine.T, d_cond, precision=HIGH)
    ada_w_grad = lax.psum_scatter(
        grad_ada.astype(jnp.bfloat16), "dp", scatter_dimension=0, tiled=True
    ).astype(jnp.float32)
    rows_qkv, rows_proj, rows_fc1, rows_fc2 = (
        lax.psum_scatter(
            grad_qkv.astype(jnp.bfloat16), "dp", scatter_dimension=0, tiled=True
        ).astype(jnp.float32),
        lax.psum_scatter(
            grad_proj.astype(jnp.bfloat16), "dp", scatter_dimension=0, tiled=True
        ).astype(jnp.float32),
        lax.psum_scatter(
            grad_fc1.astype(jnp.bfloat16), "dp", scatter_dimension=0, tiled=True
        ).astype(jnp.float32),
        lax.psum_scatter(
            grad_fc2.astype(jnp.bfloat16), "dp", scatter_dimension=0, tiled=True
        ).astype(jnp.float32),
    )
    qkv_w_grad, proj_w_grad, fc1_w_grad, fc2_w_grad = (
        lax.psum_scatter(
            rows_qkv.astype(jnp.bfloat16), "seq", scatter_dimension=1, tiled=True
        ).astype(jnp.float32),
        lax.psum_scatter(
            rows_proj.astype(jnp.bfloat16), "seq", scatter_dimension=1, tiled=True
        ).astype(jnp.float32),
        lax.psum_scatter(
            rows_fc1.astype(jnp.bfloat16), "seq", scatter_dimension=1, tiled=True
        ).astype(jnp.float32),
        lax.psum_scatter(
            rows_fc2.astype(jnp.bfloat16), "seq", scatter_dimension=1, tiled=True
        ).astype(jnp.float32),
    )
    summed = lax.psum(
        (loss_sum, bias_ada, bias_qv, bias_proj, bias_fc1, bias_fc2, grad_cond), ("dp", "seq")
    )
    loss = summed[0] / divisor
    block_out = jnp.stack(results, axis=0)
    latents_grad = jnp.stack(input_grads, axis=0)
    return (
        block_out,
        latents_grad,
        loss,
        summed[6],
        ada_w_grad,
        summed[1],
        qkv_w_grad,
        summed[2],
        proj_w_grad,
        summed[3],
        fc1_w_grad,
        summed[4],
        fc2_w_grad,
        summed[5],
    )


def solution(mesh):
    placed = (
        P(None, "dp", "seq", None),
        P(),
        P(),
        P(),
        P(None, "dp", "seq", None),
        P(None, "dp", "seq", None),
        P("dp", "seq"),
        P(),
        P("dp", "seq"),
        P(),
        P("dp", "seq"),
        P(),
        P("dp", "seq"),
        P(),
        P("dp", "seq"),
        P(),
    )
    return jax.shard_map(
        local,
        mesh=mesh,
        in_specs=placed,
        out_specs=(
            P(None, "dp", "seq", None),
            P(None, "dp", "seq", None),
            P(),
            P(),
            P("dp", "seq"),
            P(),
            P("dp", "seq"),
            P(),
            P("dp", "seq"),
            P(),
            P("dp", "seq"),
            P(),
            P("dp", "seq"),
            P(),
        ),
        check_vma=False,
    )
```

profile of v0, /device:TPU:8, one launch (start us, length us, event | category | flops | bytes accessed | tf_op | source)
XLA Modules:
  0.0 1624.2 jit_solution(10174713782407896748)
XLA Ops:
  7.3 16.6 %all_gather.52 = bf16[72,6912]{1,0:T(8,128)(2,1)} all-gather(bf16[72,3456]{1,0:T(8,128)(2,1)} %param.22), channel_id=1, replica_groups=mesh['dp'=16,'seq'=2] {'seq'}, dimensions={1}, use_global_device_ids=true | all-gather | bytes 1492992 | tf_op jit(solution)/shard_map/all_gather | solution.py:82
  40.4 103.6 %all-gather.13.cloned.1.call-done = bf16[1152,6912]{1,0:T(8,128)(2,1)} async-done(((bf16[72,6912]{1,0:T(8,128)(2,1)}), bf16[1152,6912]{1,0:T(8,128)(2,1)}) %all-gather.13.cloned.1.call-update) | async-done | bytes 15925264 | tf_op jit(solution)/shard_map/all_gather | solution.py:83
  156.9 61.6 %all-gather.15.cloned.1.call-done = bf16[1152,3456]{1,0:T(8,128)(2,1)} async-done(((bf16[72,3456]{1,0:T(8,128)(2,1)}), bf16[1152,3456]{1,0:T(8,128)(2,1)}) %all-gather.15.cloned.1.call-update) | async-done | bytes 7962640 | tf_op jit(solution)/shard_map/all_gather | solution.py:78
  256.4 17.8 %all_gather.60 = bf16[72,4608]{1,0:T(8,128)(2,1)} all-gather(bf16[72,2304]{1,0:T(8,128)(2,1)S(1)} %copy-done.31), channel_id=1, replica_groups=mesh['dp'=16,'seq'=2] {'seq'}, dimensions={1}, use_global_device_ids=true | all-gather | bytes 995328 | tf_op jit(solution)/shard_map/all_gather | solution.py:76
  297.4 15.1 all-gather.27.cloned.1.call-done
  316.8 33.2 %all-gather.17.cloned.1.call-done = bf16[1,1024,1152]{2,1,0:T(8,128)(2,1)} async-done(((bf16[1,512,1152]{2,1,0:T(8,128)(2,1)}), bf16[1,1024,1152]{2,1,0:T(8,128)(2,1)}) %all-gather.17.cloned.1.call-update) | async-done | bytes 2359312 | tf_op jit(solution)/shard_map/all_gather | solution.py:114
  354.3 33.2 %all-gather.19.cloned.1.call-done = bf16[1,1024,1152]{2,1,0:T(8,128)(2,1)} async-done(((bf16[1,512,1152]{2,1,0:T(8,128)(2,1)}), bf16[1,1024,1152]{2,1,0:T(8,128)(2,1)}) %all-gather.19.cloned.1.call-update) | async-done | bytes 2359312 | tf_op jit(solution)/shard_map/all_gather | solution.py:113
  391.8 17.5 %fusion.192 = (f32[16,512]{1,0:T(8,128)S(1)}, f32[16,512,1024]{2,1,0:T(8,128)}) fusion(bf16[512,16,72]{0,2,1:T(8,128)(2,1)} %bitcast.285, bf16[1024,16,72]{0,2,1:T(8,128)(2,1)} %bitcast.281), kind=kOutput, calls=%fused_computation.324 | convolution fusion | flops 1233126400 | bytes 37126144 | tf_op jit(solution)/shard_map/sub | solution.py:125
  409.3 15.5 fusion.97
  438.8 17.6 %fusion.191 = (f32[16,512]{1,0:T(8,128)S(1)}, f32[16,512,1024]{2,1,0:T(8,128)}) fusion(bf16[512,16,72]{0,2,1:T(8,128)(2,1)} %bitcast.287, bf16[1024,16,72]{0,2,1:T(8,128)(2,1)} %bitcast.283), kind=kOutput, calls=%fused_computation.323 | convolution fusion | flops 1233126400 | bytes 37126144 | tf_op jit(solution)/shard_map/sub | solution.py:125
  456.5 15.2 fusion.94
  481.7 40.6 %all-gather.23.cloned.1.call-done = bf16[1152,4608]{1,0:T(8,128)(2,1)} async-done(((bf16[72,4608]{1,0:T(8,128)(2,1)}), bf16[1152,4608]{1,0:T(8,128)(2,1)}) %all-gather.23.cloned.1.call-update) | async-done | bytes 10616848 | tf_op jit(solution)/shard_map/all_gather | solution.py:80
  544.2 67.8 %all-gather.25.cloned.1.call-done = bf16[4608,1152]{1,0:T(8,128)(2,1)} async-done(((bf16[288,1152]{1,0:T(8,128)(2,1)}), bf16[4608,1152]{1,0:T(8,128)(2,1)}) %all-gather.25.cloned.1.call-update) | async-done | bytes 10616848 | tf_op jit(solution)/shard_map/all_gather | solution.py:81
  625.9 20.5 %convert_reduce_fusion.5 = (f32[1152]{0:T(1024)}, bf16[512,1152]{1,0:T(8,128)(2,1)}, f32[512,1152]{1,0:T(8,128)}, f32[512,1152]{1,0:T(8,128)}, f32[1152]{0:T(102...) fusion(f32[1152]{0:T(1024)S(1)} %copy-done.92, ...), kind=kOutput, calls=%fused_computation.144 | convolution fusion | flops 5475334144 | bytes 46047756 | tf_op jit(solution)/shard_map/btf,fd->btd/dot_general | solution.py:134
  659.7 25.6 %convert_reduce_fusion.1 = (f32[4608]{0:T(1024)}, bf16[512,4608]{1,0:T(8,128)(2,1)}, f32[4608]{0:T(1024)}, bf16[512,4608]{1,0:T(8,128)(2,1)S(1)}) fusion(f32[512,4608]{1,0:T(8,128)} %fusion.171, f32[4608]{0:T(1024)S(1)} %copy-done.100, f32[512,4608]{1,0:T(8,128)} %fusion.194, f32[512,4608]{1,0:T(8,128)} %fusion.172, bf16[512,1152]{1,0:T(8,128)(2,1)S(1)} %copy-done.106, ...), kind=kOutput, calls=%fused_computation.43 | convolution fusion | flops 5544336384 | bytes 49600512 | tf_op jit(solution)/shard_map/btd,fd->btf/dot_general | solution.py:145
  742.2 23.2 %multiply_reduce_fusion.1 = (f32[16,512]{1,0:T(8,128)S(1)}, f32[16,512,1024]{2,1,0:T(8,128)}) fusion(f32[16,512,1024]{2,1,0:T(8,128)} %get-tuple-element.114, f32[16,512]{1,0:T(8,128)S(1)} %copy-done.46, bf16[512,16,72]{0,2,1:T(8,128)(2,1)} %bitcast.312, bf16[1024,16,72]{0,2,1:T(8,128)(2,1)} %bitcast.301), kind=kOutput, calls=%fused_computation.5 | convolution fusion | flops 1233117184 | bytes 70713344 | tf_op jit(solution)/shard_map/bqhe,bkhe->bhqk/dot_general | solution.py:170
  785.0 28.2 %multiply_convert_fusion.1 = bf16[16,512,1024]{2,1,0:T(8,128)(2,1)} fusion(f32[16,512,1024]{2,1,0:T(8,128)} %get-tuple-element.121, f32[16,512]{1,0:T(8,128)S(1)} %get-tuple-element.120, f32[16,512,1024]{2,1,0:T(8,128)} %get-tuple-element.114, f32[16,512]{1,0:T(8,128)S(1)} %copy-done.46), kind=kLoop, calls=%fused_computation.4 | loop fusion | flops 33554432 | bytes 83951616 | tf_op jit(solution)/shard_map/convert_element_type | solution.py:172
  824.4 14.6 fusion.91
  839.0 22.9 %multiply_reduce_fusion = (f32[16,512]{1,0:T(8,128)S(1)}, f32[16,512,1024]{2,1,0:T(8,128)}) fusion(f32[16,512,1024]{2,1,0:T(8,128)} %get-tuple-element.116, f32[16,512]{1,0:T(8,128)S(1)} %copy-done.44, bf16[512,16,72]{0,2,1:T(8,128)(2,1)} %bitcast.311, bf16[1024,16,72]{0,2,1:T(8,128)(2,1)S(1)} %bitcast.299), kind=kOutput, calls=%fused_computation.3 | convolution fusion | flops 1233117184 | bytes 70713344 | tf_op jit(solution)/shard_map/bqhe,bkhe->bhqk/dot_general | solution.py:170
  862.0 28.2 %multiply_convert_fusion = bf16[16,512,1024]{2,1,0:T(8,128)(2,1)} fusion(f32[16,512,1024]{2,1,0:T(8,128)} %get-tuple-element.126, f32[16,512]{1,0:T(8,128)S(1)} %get-tuple-element.125, f32[16,512,1024]{2,1,0:T(8,128)} %get-tuple-element.116, f32[16,512]{1,0:T(8,128)S(1)} %copy-done.44), kind=kLoop, calls=%fused_computation.2 | loop fusion | flops 33554432 | bytes 83951616 | tf_op jit(solution)/shard_map/convert_element_type | solution.py:172
  916.2 17.1 %fusion.9 = bf16[4608,1152]{1,0:T(8,128)(2,1)} fusion(f32[4608,1152]{1,0:T(8,128)} %fusion.173, bf16[512,1152]{1,0:T(8,128)(2,1)S(1)} %copy-done.105, f32[512,4608]{1,0:T(8,128)} %fusion.172, f32[4608]{0:T(1024)S(1)} %copy-done.101), kind=kOutput, calls=%fused_computation.15 | convolution fusion | flops 5470027776 | bytes 42485760 | tf_op jit(solution)/shard_map/btf,btd->fd/dot_general | solution.py:143
  947.0 16.2 fusion.8
  1007.2 14.9 fusion.12
  1048.1 16.8 %all-reduce.4 = (bf16[1,6912]{1,0:T(2,128)(2,1)S(1)}, bf16[1,6912]{1,0:T(2,128)(2,1)S(1)}) all-reduce(f32[1,6912]{1,0:T(1,128)S(1)} %constant_dynamic-update-slice_fusion.6, f32[1,6912]{1,0:T(1,128)S(1)} %constant_dynamic-update-slice_fusion), channel_id=1, replica_groups=mesh['dp'=16,'seq'=2] {'seq'}, use_global_device_ids=true, to_apply=%region_43.44 | all-reduce | flops 13824 | bytes 82944 | tf_op jit(solution)/shard_map/psum | solution.py:209
  1079.1 122.1 %reduce-scatter.34.cloned.1.call-done = bf16[72,4608]{1,0:T(8,128)(2,1)} async-done(((bf16[1152,4608]{1,0:T(8,128)(2,1)}), bf16[72,4608]{1,0:T(8,128)(2,1)}) %reduce-scatter.34.cloned.1.call-update) | async-done | bytes 663568 | tf_op jit(solution)/shard_map/reduce_scatter | solution.py:227
  1223.0 98.0 %reduce-scatter.48.cloned.1.call-done = bf16[72,3456]{1,0:T(8,128)(2,1)} async-done(((bf16[1152,3456]{1,0:T(8,128)(2,1)}), bf16[72,3456]{1,0:T(8,128)(2,1)}) %reduce-scatter.48.cloned.1.call-update) | async-done | bytes 497680
  1337.6 45.3 %all-reduce.3 = (f32[]{:T(128)}, f32[6912]{0:T(1024)}, f32[2304]{0:T(1024)}, f32[1152]{0:T(1024)}, f32[4608]{0:T(1024)}, /*index=5*/f32[1152]{0:T(1024)}) all-reduce(f32[]{:T(128)S(6)} %add.469, f32[6912]{0:T(1024)S(1)} %select_add_fusion, f32[2304]{0:T(1024)S(1)} %maximum_add_fusion, ...), channel_id=1, replica_groups=mesh['dp'=16,'seq'=2] {'dp','seq'}, use_global_device_ids=true, to_apply=%region_29.30 | all-reduce | flops 16129 | bytes 129032 | tf_op jit(solution)/shard_map/psum | solution.py:248
  1383.6 42.7 %reduce-scatter.46.cloned.1.call-done = bf16[72,3456]{1,0:T(8,128)(2,1)} async-done(((bf16[1152,3456]{1,0:T(8,128)(2,1)}), bf16[72,3456]{1,0:T(8,128)(2,1)}) %reduce-scatter.46.cloned.1.call-update) | async-done | bytes 497680
  1428.4 18.5 %reduce-scatter.44.cloned.1.call-done = bf16[576,288]{1,0:T(8,128)(2,1)} async-done(((bf16[1152,288]{1,0:T(8,128)(2,1)}), bf16[576,288]{1,0:T(8,128)(2,1)}) %reduce-scatter.44.cloned.1.call-update) | async-done | bytes 331792
  1449.0 16.3 %reduce-scatter.36.cloned.1.call-done = bf16[72,2304]{1,0:T(8,128)(2,1)} async-done(((bf16[72,4608]{1,0:T(8,128)(2,1)}), bf16[72,2304]{1,0:T(8,128)(2,1)}) %reduce-scatter.36.cloned.1.call-update) | async-done | bytes 331792 | tf_op jit(solution)/shard_map/reduce_scatter | solution.py:241
  1467.1 19.0 %reduce-scatter.40.cloned.1.call-done = bf16[1728,72]{1,0:T(8,128)(2,1)} async-done(((bf16[3456,72]{1,0:T(8,128)(2,1)}), bf16[1728,72]{1,0:T(8,128)(2,1)}) %reduce-scatter.40.cloned.1.call-update) | async-done | bytes 248848
  1488.1 126.6 %all-reduce.7.cloned.1.call-done = f32[24,1152]{1,0:T(8,128)} async-done(((f32[24,1152]{1,0:T(8,128)}), f32[24,1152]{1,0:T(8,128)}) %all-reduce.7.cloned.1.call-update) | async-done | bytes 110608 | tf_op jit(solution)/shard_map/psum | solution.py:248
  (414 shorter events, 432.7 us)
Async XLA Ops:
  7.2 136.8 %all-gather.13.cloned.1.call-start = ((), (), s32[]{:S(2)}) async-start(), calls=%async_computation.13 | async-start | bytes 16920576 | tf_op jit(solution)/shard_map/all_gather | solution.py:83
  23.9 194.6 %all-gather.15.cloned.1.call-start = ((), (), s32[]{:S(2)}) async-start(), calls=%async_computation.14 | async-start | bytes 8460288 | tf_op jit(solution)/shard_map/all_gather | solution.py:78
  33.8 259.4 %all-gather.29.cloned.1.call-start = ((), (), s32[]{:S(2)}) async-start(), calls=%async_computation.21 | async-start | bytes 3538944 | tf_op jit(solution)/shard_map/all_gather | solution.py:113
  39.0 192.0 %copy-start.69 = (f32[512]{0:T(512)}, f32[512]{0:T(512)S(1)}, u32[]{:S(2)}) copy-start(f32[512]{0:T(512)S(1)} %get-tuple-element.137) | copy-start | bytes 6148
  156.9 378.2 %copy-start.87 = (f32[1152]{0:T(1024)}, f32[1152]{0:T(1024)S(1)}, u32[]{:S(2)}) copy-start(f32[1152]{0:T(1024)S(1)} %get-tuple-element.40) | copy-start | bytes 13828
  156.9 555.9 %copy-start.50 = (f32[1152]{0:T(1024)}, f32[1152]{0:T(1024)S(1)}, u32[]{:S(2)}) copy-start(f32[1152]{0:T(1024)S(1)} %get-tuple-element.41) | copy-start | bytes 13828
  230.4 82.2 %all-gather.27.cloned.1.call-start = ((), (), s32[]{:S(2)}) async-start(), calls=%async_computation.20 | async-start | bytes 3538944 | tf_op jit(solution)/shard_map/all_gather | solution.py:114
  231.0 291.2 %copy-start.89 = (f32[1152]{0:T(1024)}, f32[1152]{0:T(1024)S(1)}, u32[]{:S(2)}) copy-start(f32[1152]{0:T(1024)S(1)} %get-tuple-element.34) | copy-start | bytes 13828
  231.0 481.1 %copy-start.53 = (f32[1152]{0:T(1024)}, f32[1152]{0:T(1024)S(1)}, u32[]{:S(2)}) copy-start(f32[1152]{0:T(1024)S(1)} %get-tuple-element.35) | copy-start | bytes 13828
  243.4 106.6 %all-gather.17.cloned.1.call-start = ((), (), s32[]{:S(2)}) async-start(), calls=%async_computation.15 | async-start | bytes 3538944 | tf_op jit(solution)/shard_map/all_gather | solution.py:114
  244.0 143.5 %all-gather.19.cloned.1.call-start = ((), (), s32[]{:S(2)}) async-start(), calls=%async_computation.16 | async-start | bytes 3538944 | tf_op jit(solution)/shard_map/all_gather | solution.py:113
  246.9 186.5 %all-gather.21.cloned.1.call-start = ((), (), s32[]{:S(2)}) async-start(), calls=%async_computation.17 | async-start | bytes 2820096 | tf_op jit(solution)/shard_map/all_gather | solution.py:79
  256.4 265.9 %all-gather.23.cloned.1.call-start = ((), (), s32[]{:S(2)}) async-start(), calls=%async_computation.18 | async-start | bytes 11280384 | tf_op jit(solution)/shard_map/all_gather | solution.py:80
  274.3 337.7 %all-gather.25.cloned.1.call-start = ((), (), s32[]{:S(2)}) async-start(), calls=%async_computation.19 | async-start | bytes 11280384 | tf_op jit(solution)/shard_map/all_gather | solution.py:81
  286.3 706.0 %reduce-scatter.50.cloned.1.call-start = ((), (), s32[]{:S(2)}) async-start(), calls=%async_computation.35 | async-start | bytes 2820096
  479.5 233.4 %copy-start.65 = (f32[512]{0:T(512)}, f32[512]{0:T(512)S(1)}, u32[]{:S(2)}) copy-start(f32[512]{0:T(512)S(1)} %broadcast_multiply_fusion) | copy-start | bytes 6148
  479.8 232.3 %copy-start.67 = (f32[512]{0:T(512)}, f32[512]{0:T(512)S(1)}, u32[]{:S(2)}) copy-start(f32[512]{0:T(512)S(1)} %broadcast_multiply_fusion.2) | copy-start | bytes 6148
  481.6 231.2 %copy-start.77 = (f32[512]{0:T(512)}, f32[512]{0:T(512)S(1)}, u32[]{:S(2)}) copy-start(f32[512]{0:T(512)S(1)} %fusion.155) | copy-start | bytes 6148
  481.6 230.5 %copy-start.79 = (f32[512]{0:T(512)}, f32[512]{0:T(512)S(1)}, u32[]{:S(2)}) copy-start(f32[512]{0:T(512)S(1)} %fusion.153) | copy-start | bytes 6148
  741.5 253.1 %reduce-scatter.28.cloned.1.call-start = ((), (), s32[]{:S(2)}) async-start(), calls=%async_computation.23 | async-start | bytes 3538944 | tf_op jit(solution)/shard_map/reduce_scatter | solution.py:188
  785.0 209.7 %reduce-scatter.26.cloned.1.call-start = ((), (), s32[]{:S(2)}) async-start(), calls=%async_computation.22 | async-start | bytes 3538944 | tf_op jit(solution)/shard_map/reduce_scatter | solution.py:185
  823.6 183.5 %reduce-scatter.32.cloned.1.call-start = ((), (), s32[]{:S(2)}) async-start(), calls=%async_computation.25 | async-start | bytes 3538944 | tf_op jit(solution)/shard_map/reduce_scatter | solution.py:188
  862.0 145.2 %reduce-scatter.30.cloned.1.call-start = ((), (), s32[]{:S(2)}) async-start(), calls=%async_computation.24 | async-start | bytes 3538944 | tf_op jit(solution)/shard_map/reduce_scatter | solution.py:185
  900.6 176.1 %reduce-scatter.38.cloned.1.call-start = ((), (), s32[]{:S(2)}) async-start(), calls=%async_computation.29 | async-start | bytes 11280384 | tf_op jit(solution)/shard_map/reduce_scatter | solution.py:230
  933.5 267.7 %reduce-scatter.34.cloned.1.call-start = ((), (), s32[]{:S(2)}) async-start(), calls=%async_computation.27 | async-start | bytes 11280384 | tf_op jit(solution)/shard_map/reduce_scatter | solution.py:227
  963.2 252.5 %reduce-scatter.42.cloned.1.call-start = ((), (), s32[]{:S(2)}) async-start(), calls=%async_computation.31 | async-start | bytes 442368
  994.1 326.9 %reduce-scatter.48.cloned.1.call-start = ((), (), s32[]{:S(2)}) async-start(), calls=%async_computation.34 | async-start | bytes 8460288
  1022.1 404.2 %reduce-scatter.46.cloned.1.call-start = ((), (), s32[]{:S(2)}) async-start(), calls=%async_computation.33 | async-start | bytes 8460288
  1071.2 375.6 %reduce-scatter.44.cloned.1.call-start = ((), (), s32[]{:S(2)}) async-start(), calls=%async_computation.32 | async-start | bytes 1327104
  1079.0 386.2 %reduce-scatter.36.cloned.1.call-start = ((), (), s32[]{:S(2)}) async-start(), calls=%async_computation.28 | async-start | bytes 995328 | tf_op jit(solution)/shard_map/reduce_scatter | solution.py:241
  1201.2 284.9 %reduce-scatter.40.cloned.1.call-start = ((), (), s32[]{:S(2)}) async-start(), calls=%async_computation.30 | async-start | bytes 1327104
  1323.4 291.3 %all-reduce.7.cloned.1.call-start = ((), (), s32[]{:S(2)}) async-start(), calls=%async_computation.26 | async-start | bytes 221184 | tf_op jit(solution)/shard_map/psum | solution.py:248
  (101 other events, 2285.7 us)
Sparse Core Ops, SparseCore 0:
  24.0 119.9 all-gather.12
  146.7 71.7 all-gather.14
  230.5 43.9 all-gather.28
  276.4 36.0 all-gather.26
  313.9 36.0 all-gather.16
  351.4 36.0 all-gather.18
  390.2 43.1 all-gather.20
  435.7 86.4 all-gather.22
  525.1 86.8 all-gather.24
  741.6 62.4 reduce-scatter.49
  806.4 34.1 reduce-scatter.27
  842.7 34.7 reduce-scatter.25
  879.8 34.6 reduce-scatter.31
  917.2 34.7 reduce-scatter.29
  956.4 120.2 reduce-scatter.37
  1081.1 119.9 reduce-scatter.33
  1203.9 11.7 reduce-scatter.41
  1220.2 100.8 reduce-scatter.47
  1325.1 101.1 reduce-scatter.45
  1428.5 18.2 reduce-scatter.43
  1449.2 16.0 reduce-scatter.35
  1467.5 18.5 reduce-scatter.39
  1492.3 122.4 all-reduce.6
where the time goes:
time: 1630 us; the launch traced here: 1620 us
  waiting for transfers between devices  816 us (50%)
  matrix products  485 us (30%)
  blocking collectives  123 us (8%)
  other arithmetic  113 us (7%)
  local copies, waits for them, and re-layouts  66.1 us (4%)
  between operations  19.4 us (1%)
    unnamed x29, waiting for transfers between devices  182 us
    psum x1, waiting for transfers between devices, local(): lax.psum((loss_sum, bias_ada, bias_qv, bias_proj, bias_fc1, bias_fc2, gra...  127 us
    reduce_scatter x1, waiting for transfers between devices, local(): lax.psum_scatter(grad_fc1.astype(jnp.bfloat16), 'dp', scatter_dimension=0...  122 us
    all_gather x1, waiting for transfers between devices, local(): ada_full = lax.all_gather(ada_cols, 'dp', axis=0, tiled=True)  104 us
    all_gather x1, waiting for transfers between devices, local(): fc2_full = lax.all_gather(fc2_cols, 'dp', axis=0, tiled=True)  67.8 us
    all_gather x1, waiting for transfers between devices, local(): qkv_full = lax.all_gather(qkv_cols, 'dp', axis=0, tiled=True)  61.6 us
    convert_element_type x2, other arithmetic, local(): d_scores = (probs * (d_probs - row_inner)).astype(bf16)  56.5 us
    all_gather x2, waiting for transfers between devices, local(): lax.all_gather(values_local, 'seq', axis=1, tiled=True)  48.3 us
  transfers between devices with their start and end apart: 23, of which 17 were waited for; matrix products, arithmetic and copies ran while one was open for 31% of the time, Pallas kernels for 0%

commit v1 on v0

--- a/solution.py
+++ b/solution.py
@@ -5,6 +5,12 @@
 
 HEADS = 16
 HIGH = lax.Precision.HIGHEST
+
+
+def take_squares(page):
+    for at in ("dp", "seq"):
+        page = jax.lax.psum(page, at)
+    return page
 
 
 def layer_norm(value):
@@ -245,9 +251,7 @@
             rows_fc2.astype(jnp.bfloat16), "seq", scatter_dimension=1, tiled=True
         ).astype(jnp.float32),
     )
-    summed = lax.psum(
-        (loss_sum, bias_ada, bias_qv, bias_proj, bias_fc1, bias_fc2, grad_cond), ("dp", "seq")
-    )
+    summed = take_squares((loss_sum, bias_ada, bias_qv, bias_proj, bias_fc1, bias_fc2, grad_cond))
     loss = summed[0] / divisor
     block_out = jnp.stack(results, axis=0)
     latents_grad = jnp.stack(input_grads, axis=0)

time: 1630 us -> 1660 us (1.018)
    reduce_scatter x1, waiting for transfers between devices: 5.22 us -> 35.6 us  [local(): lax.psum_scatter(grad_fc2.astype(jnp.bfloat16), 'dp', scatter_dimension=0...]
    psum x1 -> x2, waiting for transfers between devices: 127 us -> 109 us  [take_squares(): page = jax.lax.psum(page, at)]
    psum x1 -> x2, blocking collectives: 45.3 us -> 62.1 us  [take_squares(): page = jax.lax.psum(page, at)]
    unnamed x29 -> x30, waiting for transfers between devices: 182 us -> 182 us
    unnamed x240 -> x246, local copies, waits for them, and re-layouts: 33.1 us -> 33.2 us
  transfers between devices with their start and end apart: 23 -> 24, of which waited for: 17 -> 18; matrix products, arithmetic and copies ran while one was open for 31% -> 29% of each run, Pallas kernels for 0% -> 0%
where the time goes in v1:
time: 1660 us; the launch traced here: 1650 us
  waiting for transfers between devices  829 us (50%)
  matrix products  480 us (29%)
  blocking collectives  139 us (8%)
  other arithmetic  110 us (7%)
  local copies, waits for them, and re-layouts  66.1 us (4%)
  between operations  19.9 us (1%)
    unnamed x30, waiting for transfers between devices  182 us
    reduce_scatter x1, waiting for transfers between devices, local(): lax.psum_scatter(grad_fc1.astype(jnp.bfloat16), 'dp', scatter_dimension=0...  122 us
    psum x2, waiting for transfers between devices, take_squares(): page = jax.lax.psum(page, at)  109 us
    all_gather x1, waiting for transfers between devices, local(): ada_full = lax.all_gather(ada_cols, 'dp', axis=0, tiled=True)  104 us
    all_gather x1, waiting for transfers between devices, local(): fc2_full = lax.all_gather(fc2_cols, 'dp', axis=0, tiled=True)  68.1 us
    psum x2, blocking collectives, take_squares(): page = jax.lax.psum(page, at)  62.1 us
    all_gather x1, waiting for transfers between devices, local(): qkv_full = lax.all_gather(qkv_cols, 'dp', axis=0, tiled=True)  61.6 us
    convert_element_type x2, other arithmetic, local(): d_scores = (probs * (d_probs - row_inner)).astype(bf16)  56.7 us
  transfers between devices with their start and end apart: 24, of which 18 were waited for; matrix products, arithmetic and copies ran while one was open for 29% of the time, Pallas kernels for 0%

profile of v1, /device:TPU:8, one launch (start us, length us, event | category | flops | bytes accessed | tf_op | source)
XLA Modules:
  0.0 1645.5 jit_solution(5444971359637359001)
XLA Ops:
  7.3 16.6 %all_gather.52 = bf16[72,6912]{1,0:T(8,128)(2,1)} all-gather(bf16[72,3456]{1,0:T(8,128)(2,1)} %param.22), channel_id=1, replica_groups=mesh['dp'=16,'seq'=2] {'seq'}, dimensions={1}, use_global_device_ids=true | all-gather | bytes 1492992 | tf_op jit(solution)/shard_map/all_gather | solution.py:88
  40.2 103.7 %all-gather.13.cloned.1.call-done = bf16[1152,6912]{1,0:T(8,128)(2,1)} async-done(((bf16[72,6912]{1,0:T(8,128)(2,1)}), bf16[1152,6912]{1,0:T(8,128)(2,1)}) %all-gather.13.cloned.1.call-update) | async-done | bytes 15925264 | tf_op jit(solution)/shard_map/all_gather | solution.py:89
  156.9 61.6 %all-gather.15.cloned.1.call-done = bf16[1152,3456]{1,0:T(8,128)(2,1)} async-done(((bf16[72,3456]{1,0:T(8,128)(2,1)}), bf16[1152,3456]{1,0:T(8,128)(2,1)}) %all-gather.15.cloned.1.call-update) | async-done | bytes 7962640 | tf_op jit(solution)/shard_map/all_gather | solution.py:84
  256.4 17.9 %all_gather.60 = bf16[72,4608]{1,0:T(8,128)(2,1)} all-gather(bf16[72,2304]{1,0:T(8,128)(2,1)S(1)} %copy-done.32), channel_id=1, replica_groups=mesh['dp'=16,'seq'=2] {'seq'}, dimensions={1}, use_global_device_ids=true | all-gather | bytes 995328 | tf_op jit(solution)/shard_map/all_gather | solution.py:82
  316.8 33.2 %all-gather.17.cloned.1.call-done = bf16[1,1024,1152]{2,1,0:T(8,128)(2,1)} async-done(((bf16[1,512,1152]{2,1,0:T(8,128)(2,1)}), bf16[1,1024,1152]{2,1,0:T(8,128)(2,1)}) %all-gather.17.cloned.1.call-update) | async-done | bytes 2359312 | tf_op jit(solution)/shard_map/all_gather | solution.py:120
  354.3 33.2 %all-gather.19.cloned.1.call-done = bf16[1,1024,1152]{2,1,0:T(8,128)(2,1)} async-done(((bf16[1,512,1152]{2,1,0:T(8,128)(2,1)}), bf16[1,1024,1152]{2,1,0:T(8,128)(2,1)}) %all-gather.19.cloned.1.call-update) | async-done | bytes 2359312 | tf_op jit(solution)/shard_map/all_gather | solution.py:119
  391.8 17.5 %fusion.192 = (f32[16,512]{1,0:T(8,128)S(1)}, f32[16,512,1024]{2,1,0:T(8,128)}) fusion(bf16[512,16,72]{0,2,1:T(8,128)(2,1)} %bitcast.285, bf16[1024,16,72]{0,2,1:T(8,128)(2,1)} %bitcast.281), kind=kOutput, calls=%fused_computation.324 | convolution fusion | flops 1233126400 | bytes 37126144 | tf_op jit(solution)/shard_map/sub | solution.py:131
  409.3 15.5 fusion.97
  438.9 17.7 %fusion.191 = (f32[16,512]{1,0:T(8,128)S(1)}, f32[16,512,1024]{2,1,0:T(8,128)}) fusion(bf16[512,16,72]{0,2,1:T(8,128)(2,1)} %bitcast.287, bf16[1024,16,72]{0,2,1:T(8,128)(2,1)} %bitcast.283), kind=kOutput, calls=%fused_computation.323 | convolution fusion | flops 1233126400 | bytes 37126144 | tf_op jit(solution)/shard_map/sub | solution.py:131
  481.5 40.7 %all-gather.23.cloned.1.call-done = bf16[1152,4608]{1,0:T(8,128)(2,1)} async-done(((bf16[72,4608]{1,0:T(8,128)(2,1)}), bf16[1152,4608]{1,0:T(8,128)(2,1)}) %all-gather.23.cloned.1.call-update) | async-done | bytes 10616848 | tf_op jit(solution)/shard_map/all_gather | solution.py:86
  544.0 68.1 %all-gather.25.cloned.1.call-done = bf16[4608,1152]{1,0:T(8,128)(2,1)} async-done(((bf16[288,1152]{1,0:T(8,128)(2,1)}), bf16[4608,1152]{1,0:T(8,128)(2,1)}) %all-gather.25.cloned.1.call-update) | async-done | bytes 10616848 | tf_op jit(solution)/shard_map/all_gather | solution.py:87
  625.9 21.0 %convert_reduce_fusion.5 = (f32[1152]{0:T(1024)}, bf16[512,1152]{1,0:T(8,128)(2,1)}, f32[512,1152]{1,0:T(8,128)}, f32[512,1152]{1,0:T(8,128)}, f32[1152]{0:T(102...) fusion(f32[1152]{0:T(1024)S(1)} %copy-done.98, ...), kind=kOutput, calls=%fused_computation.144 | convolution fusion | flops 5475334144 | bytes 46047756 | tf_op jit(solution)/shard_map/btf,fd->btd/dot_general | solution.py:140
  656.3 26.3 %convert_reduce_fusion.1 = (f32[4608]{0:T(1024)}, bf16[512,4608]{1,0:T(8,128)(2,1)}, f32[4608]{0:T(1024)}, bf16[512,4608]{1,0:T(8,128)(2,1)}) fusion(f32[512,4608]{1,0:T(8,128)} %fusion.171, f32[4608]{0:T(1024)S(1)} %copy-done.106, f32[512,4608]{1,0:T(8,128)S(1)} %fusion.194, f32[512,4608]{1,0:T(8,128)} %fusion.172, ...), kind=kOutput, calls=%fused_computation.43 | convolution fusion | flops 5544336384 | bytes 49600512 | tf_op jit(solution)/shard_map/btd,fd->btf/dot_general | solution.py:151
  720.8 23.2 %multiply_reduce_fusion.1 = (f32[16,512]{1,0:T(8,128)S(1)}, f32[16,512,1024]{2,1,0:T(8,128)}) fusion(f32[16,512,1024]{2,1,0:T(8,128)} %get-tuple-element.120, f32[16,512]{1,0:T(8,128)S(1)} %get-tuple-element.119, bf16[512,16,72]{0,2,1:T(8,128)(2,1)} %bitcast.313, bf16[1024,16,72]{0,2,1:T(8,128)(2,1)} %bitcast.303), kind=kOutput, calls=%fused_computation.5 | convolution fusion | flops 1233117184 | bytes 70713344 | tf_op jit(solution)/shard_map/bqhe,bkhe->bhqk/dot_general | solution.py:176
  769.5 28.2 %multiply_convert_fusion.1 = bf16[16,512,1024]{2,1,0:T(8,128)(2,1)} fusion(f32[16,512,1024]{2,1,0:T(8,128)} %get-tuple-element.127, f32[16,512]{1,0:T(8,128)S(1)} %get-tuple-element.126, f32[16,512,1024]{2,1,0:T(8,128)} %get-tuple-element.120, f32[16,512]{1,0:T(8,128)S(1)} %get-tuple-element.119), kind=kLoop, calls=%fused_computation.4 | loop fusion | flops 33554432 | bytes 83951616 | tf_op jit(solution)/shard_map/convert_element_type | solution.py:178
  808.7 15.2 fusion.91
  823.9 22.8 %multiply_reduce_fusion = (f32[16,512]{1,0:T(8,128)S(1)}, f32[16,512,1024]{2,1,0:T(8,128)}) fusion(f32[16,512,1024]{2,1,0:T(8,128)} %get-tuple-element.122, f32[16,512]{1,0:T(8,128)S(1)} %copy-done.47, bf16[512,16,72]{0,2,1:T(8,128)(2,1)} %bitcast.311, bf16[1024,16,72]{0,2,1:T(8,128)(2,1)S(1)} %bitcast.299), kind=kOutput, calls=%fused_computation.3 | convolution fusion | flops 1233117184 | bytes 70713344 | tf_op jit(solution)/shard_map/bqhe,bkhe->bhqk/dot_general | solution.py:176
  846.8 28.5 %multiply_convert_fusion = bf16[16,512,1024]{2,1,0:T(8,128)(2,1)} fusion(f32[16,512,1024]{2,1,0:T(8,128)} %get-tuple-element.132, f32[16,512]{1,0:T(8,128)S(1)} %get-tuple-element.131, f32[16,512,1024]{2,1,0:T(8,128)} %get-tuple-element.122, f32[16,512]{1,0:T(8,128)S(1)} %copy-done.47), kind=kLoop, calls=%fused_computation.2 | loop fusion | flops 33554432 | bytes 83951616 | tf_op jit(solution)/shard_map/convert_element_type | solution.py:178
  908.6 16.4 fusion.9
  938.9 16.5 %fusion.8 = bf16[1152,4608]{1,0:T(8,128)(2,1)} fusion(f32[1152,4608]{1,0:T(8,128)} %fusion.170, bf16[512,4608]{1,0:T(8,128)(2,1)} %get-tuple-element.110, f32[512,1152]{1,0:T(8,128)S(1)} %copy-done.9, f32[1152]{0:T(1024)S(1)} %copy-done.94, f32[1152]{0:T(1024)S(1)} %copy-done.54, f32[512]{0:T(512)S(1)} %copy-done.84, f32[512]{0:T(512)S(1)} %copy-done.69), kind=kOutput, calls=%fused_computation.14 | convolution fusion | flops 5449383936 | bytes 38941696 | tf_op jit(solution)/shard_map/btd,btf->df/dot_general | solution.py:153
  995.4 17.1 %fusion.12 = bf16[1152,3456]{1,0:T(8,128)(2,1)} fusion(f32[1152,3456]{1,0:T(8,128)} %fusion.101, bf16[1,512,1152]{1,2,0:T(8,128)(2,1)} %reduce-scatter.32.cloned.1.call-done, bf16[1,512,1152]{1,2,0:T(8,128)(2,1)} %reduce-scatter.30.cloned.1.call-done, bf16[1,512,1152]{1,2,0:T(8,128)(2,1)} %bitcast.305, f32[1152]{0:T(1024)S(1)} %copy-done.90, ...), kind=kOutput, calls=%fused_computation.22 | convolution fusion | flops 4098981888 | bytes 28626944 | tf_op jit(solution)/shard_map/btd,bte->de/dot_general | solution.py:200
  1041.5 16.2 all-reduce.5
  1076.2 35.6 %reduce-scatter.38.cloned.1.call-done = bf16[288,1152]{1,0:T(8,128)(2,1)} async-done(((bf16[4608,1152]{1,0:T(8,128)(2,1)}), bf16[288,1152]{1,0:T(8,128)(2,1)}) %reduce-scatter.38.cloned.1.call-update) | async-done | bytes 663568 | tf_op jit(solution)/shard_map/reduce_scatter | solution.py:236
  1114.1 122.0 %reduce-scatter.34.cloned.1.call-done = bf16[72,4608]{1,0:T(8,128)(2,1)} async-done(((bf16[1152,4608]{1,0:T(8,128)(2,1)}), bf16[72,4608]{1,0:T(8,128)(2,1)}) %reduce-scatter.34.cloned.1.call-update) | async-done | bytes 663568 | tf_op jit(solution)/shard_map/reduce_scatter | solution.py:233
  1243.5 97.7 %reduce-scatter.48.cloned.1.call-done = bf16[72,3456]{1,0:T(8,128)(2,1)} async-done(((bf16[1152,3456]{1,0:T(8,128)(2,1)}), bf16[72,3456]{1,0:T(8,128)(2,1)}) %reduce-scatter.48.cloned.1.call-update) | async-done | bytes 497680
  1360.7 87.4 %all-reduce.9.cloned.1.call-done = f32[24,1152]{1,0:T(8,128)} async-done(((f32[24,1152]{1,0:T(8,128)}), f32[24,1152]{1,0:T(8,128)}) %all-reduce.9.cloned.1.call-update) | async-done | bytes 110608 | tf_op jit(solution)/shard_map/psum | solution.py:12
  1452.6 52.0 %all-reduce.3 = (f32[]{:T(128)}, f32[6912]{0:T(1024)S(1)}, f32[2304]{0:T(1024)S(1)}, f32[1152]{0:T(1024)S(1)}, f32[4608]{0:T(1024)S(1)}, /*index=5*/f32[1152]{0:T(1024)S(1)}) all-reduce(f32[]{:T(128)S(6)} %add.483, f32[6912]{0:T(1024)S(1)} %select_add_fusion, ...), channel_id=1, replica_groups=mesh['dp'=16,'seq'=2] {'dp'}, use_global_device_ids=true, to_apply=%region_29.30 | all-reduce | flops 16129 | bytes 129032 | tf_op jit(solution)/shard_map/psum | solution.py:12
  1515.3 37.2 %reduce-scatter.46.cloned.1.call-done = bf16[72,3456]{1,0:T(8,128)(2,1)} async-done(((bf16[1152,3456]{1,0:T(8,128)(2,1)}), bf16[72,3456]{1,0:T(8,128)(2,1)}) %reduce-scatter.46.cloned.1.call-update) | async-done | bytes 497680
  1554.6 18.6 %reduce-scatter.44.cloned.1.call-done = bf16[576,288]{1,0:T(8,128)(2,1)} async-done(((bf16[1152,288]{1,0:T(8,128)(2,1)}), bf16[576,288]{1,0:T(8,128)(2,1)}) %reduce-scatter.44.cloned.1.call-update) | async-done | bytes 331792
  1575.3 16.3 reduce-scatter.36.cloned.1.call-done
  1593.5 19.0 %reduce-scatter.40.cloned.1.call-done = bf16[1728,72]{1,0:T(8,128)(2,1)} async-done(((bf16[3456,72]{1,0:T(8,128)(2,1)}), bf16[1728,72]{1,0:T(8,128)(2,1)}) %reduce-scatter.40.cloned.1.call-update) | async-done | bytes 248848
  1614.5 21.3 %all-reduce.11.cloned.1.call-done = f32[24,1152]{1,0:T(8,128)} async-done(((f32[24,1152]{1,0:T(8,128)}), f32[24,1152]{1,0:T(8,128)}) %all-reduce.11.cloned.1.call-update) | async-done | bytes 110608 | tf_op jit(solution)/shard_map/psum | solution.py:12
  (424 shorter events, 461.4 us)
Async XLA Ops:
  7.2 136.8 %all-gather.13.cloned.1.call-start = ((), (), s32[]{:S(2)}) async-start(), calls=%async_computation.13 | async-start | bytes 16920576 | tf_op jit(solution)/shard_map/all_gather | solution.py:89
  23.9 194.6 %all-gather.15.cloned.1.call-start = ((), (), s32[]{:S(2)}) async-start(), calls=%async_computation.14 | async-start | bytes 8460288 | tf_op jit(solution)/shard_map/all_gather | solution.py:84
  33.8 259.4 %all-gather.29.cloned.1.call-start = ((), (), s32[]{:S(2)}) async-start(), calls=%async_computation.21 | async-start | bytes 3538944 | tf_op jit(solution)/shard_map/all_gather | solution.py:119
  38.8 192.2 %copy-start.72 = (f32[512]{0:T(512)}, f32[512]{0:T(512)S(1)}, u32[]{:S(2)}) copy-start(f32[512]{0:T(512)S(1)} %get-tuple-element.143) | copy-start | bytes 6148
  156.9 314.7 %copy-start.35 = (f32[1152]{0:T(1024)}, f32[1152]{0:T(1024)S(1)}, u32[]{:S(2)}) copy-start(f32[1152]{0:T(1024)S(1)} %get-tuple-element.44) | copy-start | bytes 13828
  156.9 377.9 %copy-start.52 = (f32[1152]{0:T(1024)}, f32[1152]{0:T(1024)S(1)}, u32[]{:S(2)}) copy-start(f32[1152]{0:T(1024)S(1)} %get-tuple-element.41) | copy-start | bytes 13828
  156.9 377.9 %copy-start.93 = (f32[1152]{0:T(1024)}, f32[1152]{0:T(1024)S(1)}, u32[]{:S(2)}) copy-start(f32[1152]{0:T(1024)S(1)} %get-tuple-element.40) | copy-start | bytes 13828
  230.4 82.2 %all-gather.27.cloned.1.call-start = ((), (), s32[]{:S(2)}) async-start(), calls=%async_computation.20 | async-start | bytes 3538944 | tf_op jit(solution)/shard_map/all_gather | solution.py:120
  231.0 291.2 %copy-start.95 = (f32[1152]{0:T(1024)}, f32[1152]{0:T(1024)S(1)}, u32[]{:S(2)}) copy-start(f32[1152]{0:T(1024)S(1)} %get-tuple-element.34) | copy-start | bytes 13828
  231.1 464.0 %copy-start.55 = (f32[1152]{0:T(1024)}, f32[1152]{0:T(1024)S(1)}, u32[]{:S(2)}) copy-start(f32[1152]{0:T(1024)S(1)} %get-tuple-element.35) | copy-start | bytes 13828
  243.4 106.6 %all-gather.17.cloned.1.call-start = ((), (), s32[]{:S(2)}) async-start(), calls=%async_computation.15 | async-start | bytes 3538944 | tf_op jit(solution)/shard_map/all_gather | solution.py:120
  244.0 143.5 %all-gather.19.cloned.1.call-start = ((), (), s32[]{:S(2)}) async-start(), calls=%async_computation.16 | async-start | bytes 3538944 | tf_op jit(solution)/shard_map/all_gather | solution.py:119
  246.9 186.5 %all-gather.21.cloned.1.call-start = ((), (), s32[]{:S(2)}) async-start(), calls=%async_computation.17 | async-start | bytes 2820096 | tf_op jit(solution)/shard_map/all_gather | solution.py:85
  256.4 265.9 %all-gather.23.cloned.1.call-start = ((), (), s32[]{:S(2)}) async-start(), calls=%async_computation.18 | async-start | bytes 11280384 | tf_op jit(solution)/shard_map/all_gather | solution.py:86
  274.3 337.8 %all-gather.25.cloned.1.call-start = ((), (), s32[]{:S(2)}) async-start(), calls=%async_computation.19 | async-start | bytes 11280384 | tf_op jit(solution)/shard_map/all_gather | solution.py:87
  286.3 696.0 %reduce-scatter.28.cloned.1.call-start = ((), (), s32[]{:S(2)}) async-start(), calls=%async_computation.23 | async-start | bytes 3538944 | tf_op jit(solution)/shard_map/reduce_scatter | solution.py:194
  479.8 215.2 %copy-start.70 = (f32[512]{0:T(512)}, f32[512]{0:T(512)S(1)}, u32[]{:S(2)}) copy-start(f32[512]{0:T(512)S(1)} %broadcast_multiply_fusion.2) | copy-start | bytes 6148
  481.5 213.5 %copy-start.85 = (f32[512]{0:T(512)}, f32[512]{0:T(512)S(1)}, u32[]{:S(2)}) copy-start(f32[512]{0:T(512)S(1)} %fusion.153) | copy-start | bytes 6148
  769.4 212.9 %reduce-scatter.26.cloned.1.call-start = ((), (), s32[]{:S(2)}) async-start(), calls=%async_computation.22 | async-start | bytes 3538944 | tf_op jit(solution)/shard_map/reduce_scatter | solution.py:191
  808.0 187.4 %reduce-scatter.32.cloned.1.call-start = ((), (), s32[]{:S(2)}) async-start(), calls=%async_computation.25 | async-start | bytes 3538944 | tf_op jit(solution)/shard_map/reduce_scatter | solution.py:194
  846.7 148.7 %reduce-scatter.30.cloned.1.call-start = ((), (), s32[]{:S(2)}) async-start(), calls=%async_computation.24 | async-start | bytes 3538944 | tf_op jit(solution)/shard_map/reduce_scatter | solution.py:191
  885.6 128.3 %reduce-scatter.50.cloned.1.call-start = ((), (), s32[]{:S(2)}) async-start(), calls=%async_computation.36 | async-start | bytes 2820096
  892.5 219.2 %reduce-scatter.38.cloned.1.call-start = ((), (), s32[]{:S(2)}) async-start(), calls=%async_computation.30 | async-start | bytes 11280384 | tf_op jit(solution)/shard_map/reduce_scatter | solution.py:236
  925.1 311.1 %reduce-scatter.34.cloned.1.call-start = ((), (), s32[]{:S(2)}) async-start(), calls=%async_computation.28 | async-start | bytes 11280384 | tf_op jit(solution)/shard_map/reduce_scatter | solution.py:233
  955.5 385.7 %reduce-scatter.48.cloned.1.call-start = ((), (), s32[]{:S(2)}) async-start(), calls=%async_computation.35 | async-start | bytes 8460288
  1012.6 343.2 %reduce-scatter.42.cloned.1.call-start = ((), (), s32[]{:S(2)}) async-start(), calls=%async_computation.32 | async-start | bytes 442368
  1015.7 432.3 %all-reduce.9.cloned.1.call-start = ((), (), s32[]{:S(2)}) async-start(), calls=%async_computation.26 | async-start | bytes 221184 | tf_op jit(solution)/shard_map/psum | solution.py:12
  1069.8 482.7 %reduce-scatter.46.cloned.1.call-start = ((), (), s32[]{:S(2)}) async-start(), calls=%async_computation.34 | async-start | bytes 8460288
  1076.1 497.0 %reduce-scatter.44.cloned.1.call-start = ((), (), s32[]{:S(2)}) async-start(), calls=%async_computation.33 | async-start | bytes 1327104
  1114.1 477.6 %reduce-scatter.36.cloned.1.call-start = ((), (), s32[]{:S(2)}) async-start(), calls=%async_computation.29 | async-start | bytes 995328 | tf_op jit(solution)/shard_map/reduce_scatter | solution.py:247
  1236.2 376.3 %reduce-scatter.40.cloned.1.call-start = ((), (), s32[]{:S(2)}) async-start(), calls=%async_computation.31 | async-start | bytes 1327104
  1343.5 292.3 %all-reduce.11.cloned.1.call-start = ((), (), s32[]{:S(2)}) async-start(), calls=%async_computation.27 | async-start | bytes 221184 | tf_op jit(solution)/shard_map/psum | solution.py:12
  (105 other events, 2167.3 us)
Sparse Core Ops, SparseCore 0:
  24.0 119.9 all-gather.12
  146.7 71.7 all-gather.14
  230.5 43.9 all-gather.28
  276.4 36.0 all-gather.26
  313.9 36.0 all-gather.16
  351.4 36.0 all-gather.18
  390.2 43.1 all-gather.20
  435.7 86.4 all-gather.22
  525.1 86.9 all-gather.24
  769.6 33.8 reduce-scatter.27
  808.1 34.3 reduce-scatter.25
  846.8 34.3 reduce-scatter.31
  885.7 34.7 reduce-scatter.29
  924.3 63.2 reduce-scatter.49
  992.0 119.6 reduce-scatter.37
  1116.2 119.9 reduce-scatter.33
  1240.7 100.5 reduce-scatter.47
  1343.9 11.8 reduce-scatter.41
  1359.8 88.2 all-reduce.8
  1452.0 100.4 reduce-scatter.45
  1554.9 18.2 reduce-scatter.43
  1575.5 16.0 reduce-scatter.35
  1593.9 18.5 reduce-scatter.39
  1614.6 21.1 all-reduce.10
